TPU v7x, 256 devices: a whole 4x4x8 slice. The times are simulated.
256 devices in a mesh: segment: 8 (over x, core), seq: 32 (over z, y).
Axes of the slice: x: 4, y: 4, z: 8, core: 2. Of those that a mesh axis runs over, the one named last changes fastest.
Arguments:
- latent: bfloat16 [12288, 1536], P('seq'), may hold values from -4 to 4
- stale_kv: bfloat16 [8, 2, 12288, 1536], P('segment', None, 'seq'), may hold values from -3 to 3
- query_weight: bfloat16 [8, 1536, 1536], P('segment', 'seq'), may hold values from -0.15625 to 0.15625
- key_weight: bfloat16 [8, 1536, 1536], P('segment', 'seq'), may hold values from -0.15625 to 0.15625
- value_weight: bfloat16 [8, 1536, 1536], P('segment', 'seq'), may hold values from -0.15625 to 0.15625
- out_weight: bfloat16 [8, 1536, 1536], P('segment', 'seq'), may hold values from -0.3125 to 0.3125
- query_gain: float32 [8, 128], P('segment'), may hold values from 0.5 to 2
- key_gain: float32 [8, 128], P('segment'), may hold values from 0.5 to 2
- tile_mask: int32 [192, 6], P('seq'), may hold values from -1 to 191, as said below
Outputs:
- section_out: bfloat16 [8, 12288, 1536], P('segment', 'seq')
Inputs may be any that keep to these rules, and one draw needn't show every extreme that they name: `tile_mask`: row g lists the key tiles of query tile g: slot 0 holds g itself, the next slots distinct other tiles whose tile-frame (tile number // 6) differs from that of g by at most one, and the remaining slots -1. Every row lists two or more tiles, and some row lists 6.
All inputs are finite; a program needn't handle non-finite values.
Results may differ from a plain program's by a relative error of at most 0.027.
Values may be sent and summed in bfloat16 or wider, within the bound.
No kernel may reach another device: no remote copies, remote signals or barrier semaphores. Data moves between devices by JAX's collectives and lax.ppermute only.
A program may use at most 128 MiB of HBM per device.

v0:
```python
import math
import jax
import jax.numpy as jnp
from jax import lax
from jax.sharding import PartitionSpec as P

D = 1536
HEADS = 12
HEAD = 128
TILE = 64
PATCHES = 3
TPP = 2
epsilon = 1e-06


def extended(cells, sides, width):
    for axis, dim in sides:
        count = lax.axis_size(axis)
        ends = count - 1
        head = lax.slice_in_dim(cells, 0, width, axis=dim)
        tail = lax.slice_in_dim(cells, cells.shape[dim] - width, cells.shape[dim], axis=dim)
        cells = jnp.concatenate(
            [
                lax.ppermute(tail, axis, [(i, (i + 1) % count) for i in range(ends)]),
                cells,
                lax.ppermute(head, axis, [((i + 1) % count, i) for i in range(ends)]),
            ],
            axis=dim,
        )
    return cells


def from_behind(value, axis, by):
    count = lax.axis_size(axis)
    pairs = [(i, i + by) for i in range(count) if 0 <= i + by < count]
    return lax.ppermute(value, axis, pairs)


def head_normed(projected, gain):
    n_rows = projected.shape[0]
    heads = projected.reshape(n_rows, HEADS, HEAD)
    scaled = heads * lax.rsqrt(jnp.mean(heads * heads, axis=-1, keepdims=True) + epsilon)
    return (scaled * gain).reshape(n_rows, D).astype(jnp.bfloat16)


def keys_values(inputs, weight_k, weight_v, gain_k):
    keys = head_normed(jnp.dot(inputs, weight_k, preferred_element_type=jnp.float32), gain_k)
    values = jnp.dot(inputs, weight_v, preferred_element_type=jnp.float32).astype(jnp.bfloat16)
    return jnp.stack([keys, values])


def attend(queries, blocks, tile_index, usable):
    n_query = tile_index.shape[0]
    key_heads = jnp.take(blocks[0], tile_index, axis=0).reshape(n_query, -1, HEADS, HEAD)
    value_heads = jnp.take(blocks[1], tile_index, axis=0).reshape(n_query, -1, HEADS, HEAD)
    query_heads = queries.reshape(n_query, -1, HEADS, HEAD)
    scores = jnp.einsum(
        "pthe,pkhe->phtk", query_heads, key_heads, preferred_element_type=jnp.float32
    ) / math.sqrt(HEAD)
    listed = jnp.repeat(usable, TILE, axis=1).astype(jnp.float32)
    weights = jnp.exp(scores) * listed[:, None, None, :]
    totals = jnp.sum(weights, axis=-1)
    summed = jnp.einsum(
        "phtk,pkhe->pthe",
        weights.astype(jnp.bfloat16),
        value_heads,
        preferred_element_type=jnp.float32,
    )
    return summed / jnp.swapaxes(totals, 1, 2)[..., None]


def per_device(
    latent,
    stale_kv,
    query_weight,
    key_weight,
    value_weight,
    out_weight,
    query_gain,
    key_gain,
    tile_mask,
):
    tok_dev = latent.shape[0]
    patch_rows = tok_dev // PATCHES
    tiles_dev = tile_mask.shape[0]
    segment_id = lax.axis_index("segment")
    frame_id = lax.axis_index("seq")
    rounds = PATCHES + lax.axis_size("segment") - 1
    full_q, full_k, full_v, full_out = (
        lax.all_gather(query_weight[0], "seq", axis=0, tiled=True),
        lax.all_gather(key_weight[0], "seq", axis=0, tiled=True),
        lax.all_gather(value_weight[0], "seq", axis=0, tiled=True),
        lax.all_gather(out_weight[0], "seq", axis=0, tiled=True),
    )
    gain_q = query_gain[0]
    gain_k = key_gain[0]
    local_kv = stale_kv[0]
    window = extended(local_kv, (("seq", 1),), tok_dev)
    zero_rows = jnp.zeros((patch_rows, D), jnp.bfloat16)
    zero_pair = jnp.zeros((2, patch_rows, D), jnp.bfloat16)

    def project(inputs):
        fresh_q = head_normed(jnp.dot(inputs, full_q, preferred_element_type=jnp.float32), gain_q)
        return (fresh_q, keys_values(inputs, full_k, full_v, gain_k))

    def skip_project(inputs):
        return (zero_rows, zero_pair)

    def advance(round_id, carry):
        window, received, result = carry
        patch_id = round_id - segment_id
        active = (patch_id >= 0) & (patch_id < PATCHES)
        current = jnp.clip(patch_id, 0, PATCHES - 1)
        offset = current * patch_rows
        entering = lax.dynamic_slice_in_dim(latent, offset, patch_rows, 0)
        inputs = jnp.where(segment_id == 0, entering, received)
        fresh_q, own_kv = lax.cond(active, project, skip_project, inputs)
        spread = extended(own_kv, (("seq", 1),), patch_rows)
        trailing = spread[:, :patch_rows]
        leading = spread[:, 2 * patch_rows :]

        def finish(state):
            former, stored = state
            updated = lax.dynamic_update_slice_in_dim(former, trailing, offset, 1)
            updated = lax.dynamic_update_slice_in_dim(updated, own_kv, tok_dev + offset, 1)
            updated = lax.dynamic_update_slice_in_dim(updated, leading, 2 * tok_dev + offset, 1)
            listing = lax.dynamic_slice_in_dim(tile_mask, current * TPP, TPP, 0)
            usable = listing >= 0
            tile_index = jnp.where(usable, listing - (frame_id - 1) * tiles_dev, 0)
            blocks = updated.reshape(2, 3 * tiles_dev, TILE, D)
            attention = attend(fresh_q.reshape(TPP, TILE, D), blocks, tile_index, usable)
            attention_b = attention.reshape(patch_rows, D).astype(jnp.bfloat16)
            mixed = jnp.dot(attention_b, full_out, preferred_element_type=jnp.float32)
            leaving = (inputs.astype(jnp.float32) + mixed).astype(jnp.bfloat16)
            stored = lax.dynamic_update_slice_in_dim(stored, leaving, offset, 0)
            return (updated, stored, leaving)

        def remain(state):
            return (state[0], state[1], zero_rows)

        window, result, leaving = lax.cond(active, finish, remain, (window, result))
        received = from_behind(leaving, "segment", 1)
        return (window, received, result)

    initial = (window, zero_rows, jnp.zeros((tok_dev, D), jnp.bfloat16))
    final_state = lax.fori_loop(0, rounds, advance, initial)
    return final_state[2][None]


def solution(mesh):
    return jax.shard_map(
        per_device,
        mesh=mesh,
        in_specs=(
            P("seq", None),
            P("segment", None, "seq", None),
            P("segment", "seq", None),
            P("segment", "seq", None),
            P("segment", "seq", None),
            P("segment", "seq", None),
            P("segment", None),
            P("segment", None),
            P("seq", None),
        ),
        out_specs=P("segment", "seq", None),
        check_vma=False,
    )
```

profile of v0, /device:TPU:127, one launch (start us, length us, event | category | flops | bytes accessed | tf_op | source)
XLA Modules:
  0.0 1289.9 jit_solution(12764874456746758375)
XLA Ops:
  15.7 59.3 %collective-permute-done.3 = bf16[2,384,1536]{2,1,0:T(8,128)(2,1)S(1)} collective-permute-done((bf16[2,384,1536]{2,1,0:T(8,128)(2,1)}, bf16[2,384,1536]{2,1,0:T(8,128)(2,1)S(1)}, u32[]{:S(2)}, u32[]{:S(2)}) %collective-permute-start.3) | collective-permute-done | bytes 2359328 | tf_op jit(solution)/shard_map/ppermute | solution.py:24
  88.6 15.1 %all-gather.9.cloned.1.call-done = bf16[1,1536,1536]{2,1,0:T(8,128)(2,1)} async-done(((bf16[1,48,1536]{2,1,0:T(8,128)(2,1)}), bf16[1,1536,1536]{2,1,0:T(8,128)(2,1)}) %all-gather.9.cloned.1.call-update) | async-done | bytes 4718608 | tf_op jit(solution)/shard_map/all_gather | solution.py:90
  103.7 81.8 %all-gather.11.cloned.1.call-done = bf16[1,1536,1536]{2,1,0:T(8,128)(2,1)} async-done(((bf16[1,48,1536]{2,1,0:T(8,128)(2,1)}), bf16[1,1536,1536]{2,1,0:T(8,128)(2,1)}) %all-gather.11.cloned.1.call-update) | async-done | bytes 4718608 | tf_op jit(solution)/shard_map/all_gather | solution.py:91
  185.4 83.4 %all-gather.13.cloned.1.call-done = bf16[1,1536,1536]{2,1,0:T(8,128)(2,1)} async-done(((bf16[1,48,1536]{2,1,0:T(8,128)(2,1)}), bf16[1,1536,1536]{2,1,0:T(8,128)(2,1)}) %all-gather.13.cloned.1.call-update) | async-done | bytes 4718608 | tf_op jit(solution)/shard_map/all_gather | solution.py:92
  268.9 83.3 %all-gather.15.cloned.1.call-done = bf16[1,1536,1536]{2,1,0:T(8,128)(2,1)} async-done(((bf16[1,48,1536]{2,1,0:T(8,128)(2,1)}), bf16[1,1536,1536]{2,1,0:T(8,128)(2,1)}) %all-gather.15.cloned.1.call-update) | async-done | bytes 4718608 | tf_op jit(solution)/shard_map/all_gather | solution.py:93
  353.3 930.1 %while.18 = (s32[]{:T(128)}, bf16[2,1152,1536]{2,1,0:T(8,128)(2,1)}, bf16[128,1536]{1,0:T(8,128)(2,1)S(1)}, bf16[384,1536]{1,0:T(8,128)(2,1)}, s32[]{:T(128)}, /...) while((s32[]{:T(128)}, ...), condition=%wide.region_8.10_spmd, body=%wide.region_0.9_spmd.sunk | while | flops 2727545344 | bytes 147957200 | solution.py:146
  360.9 11.2 collective-permute-done
  394.7 9.7 collective-permute-done
  443.0 10.0 collective-permute-done.2
  459.6 9.7 collective-permute-done
  476.5 8.9 collective-permute-done.2
  492.0 9.7 collective-permute-done
  524.4 9.7 collective-permute-done
  541.4 8.9 collective-permute-done.2
  571.5 419.4 %collective-permute-done.2 = bf16[128,1536]{1,0:T(8,128)(2,1)S(1)} collective-permute-done((bf16[128,1536]{1,0:T(8,128)(2,1)}, bf16[128,1536]{1,0:T(8,128)(2,1)S(1)}, u32[]{:S(2)}, u32[]{:S(2)}) %collective-permute-start.2) | collective-permute-done | bytes 393248 | tf_op jit(solution)/shard_map/while/body/eval_jaxpr/ppermute | solution.py:36
  992.1 9.9 conditional.4
  1020.0 54.0 %conditional.5 = (bf16[2,1152,1536]{2,1,0:T(8,128)(2,1)}, bf16[384,1536]{1,0:T(8,128)(2,1)}, bf16[128,1536]{1,0:T(8,128)(2,1)}) conditional(s32[]{:T(128)} %convert_element_type.58, (bf16[2,1152,1536]{2,1,0:T(8,128)(2,1)}, bf16[384,1536]{1,0:T(8,128)(2,1)}) %tuple.60, (s32[]{:T(128)}, bf16[2,1152,1536]{2,1,0:T(8,128)(2,1)}, ...), branch_computations={%region_5.5_spmd, %region_6.8_spmd} | conditional | flops 912850560 | bytes 86146920 | solution.py:141
  1075.3 14.0 %collective-permute-done.2 = bf16[128,1536]{1,0:T(8,128)(2,1)S(1)} collective-permute-done((bf16[128,1536]{1,0:T(8,128)(2,1)}, bf16[128,1536]{1,0:T(8,128)(2,1)S(1)}, u32[]{:S(2)}, u32[]{:S(2)}) %collective-permute-start.2) | collective-permute-done | bytes 393248 | tf_op jit(solution)/shard_map/while/body/eval_jaxpr/ppermute | solution.py:36
  1090.3 9.9 conditional.4
  1118.2 54.0 %conditional.5 = (bf16[2,1152,1536]{2,1,0:T(8,128)(2,1)}, bf16[384,1536]{1,0:T(8,128)(2,1)}, bf16[128,1536]{1,0:T(8,128)(2,1)}) conditional(s32[]{:T(128)} %convert_element_type.58, (bf16[2,1152,1536]{2,1,0:T(8,128)(2,1)}, bf16[384,1536]{1,0:T(8,128)(2,1)}) %tuple.60, (s32[]{:T(128)}, bf16[2,1152,1536]{2,1,0:T(8,128)(2,1)}, ...), branch_computations={%region_5.5_spmd, %region_6.8_spmd} | conditional | flops 912850560 | bytes 86146920 | solution.py:141
  1173.6 18.1 %collective-permute-done.2 = bf16[128,1536]{1,0:T(8,128)(2,1)S(1)} collective-permute-done((bf16[128,1536]{1,0:T(8,128)(2,1)}, bf16[128,1536]{1,0:T(8,128)(2,1)S(1)}, u32[]{:S(2)}, u32[]{:S(2)}) %collective-permute-start.2) | collective-permute-done | bytes 393248 | tf_op jit(solution)/shard_map/while/body/eval_jaxpr/ppermute | solution.py:36
  1192.7 9.9 conditional.4
  1208.0 12.8 collective-permute-done
  1225.7 53.8 %conditional.5 = (bf16[2,1152,1536]{2,1,0:T(8,128)(2,1)}, bf16[384,1536]{1,0:T(8,128)(2,1)}, bf16[128,1536]{1,0:T(8,128)(2,1)}) conditional(s32[]{:T(128)} %convert_element_type.58, (bf16[2,1152,1536]{2,1,0:T(8,128)(2,1)}, bf16[384,1536]{1,0:T(8,128)(2,1)}) %tuple.60, (s32[]{:T(128)}, bf16[2,1152,1536]{2,1,0:T(8,128)(2,1)}, ...), branch_computations={%region_5.5_spmd, %region_6.8_spmd} | conditional | flops 912850560 | bytes 86146920 | solution.py:141
  (268 shorter events, 416.8 us)
Async XLA Ops:
  6.5 97.1 %all-gather.9.cloned.1.call-start = ((), (), s32[]{:S(2)}) async-start(), calls=%async_computation | async-start | bytes 4866048 | tf_op jit(solution)/shard_map/all_gather | solution.py:90
  7.3 178.2 %all-gather.11.cloned.1.call-start = ((), (), s32[]{:S(2)}) async-start(), calls=%async_computation.1 | async-start | bytes 4866048 | tf_op jit(solution)/shard_map/all_gather | solution.py:91
  8.0 260.9 %all-gather.13.cloned.1.call-start = ((), (), s32[]{:S(2)}) async-start(), calls=%async_computation.2 | async-start | bytes 4866048 | tf_op jit(solution)/shard_map/all_gather | solution.py:92
  8.7 343.4 %all-gather.15.cloned.1.call-start = ((), (), s32[]{:S(2)}) async-start(), calls=%async_computation.3 | async-start | bytes 4866048 | tf_op jit(solution)/shard_map/all_gather | solution.py:93
  9.3 65.7 %collective-permute-start.3 = (bf16[2,384,1536]{2,1,0:T(8,128)(2,1)}, bf16[2,384,1536]{2,1,0:T(8,128)(2,1)S(1)}, u32[]{:S(2)}, u32[]{:S(2)}) collective-permute-start(bf16[2,384,1536]{2,1,0:T(8,128)(2,1)} %bitcast.66), channel_id=1, source_target_pairs={{0,1},{1,2},{2,3},{3,4},{4,5},{5,6},{6,7},{7,8},{8,9},{9,10},{10,1... | collective-permute-start | bytes 7077896 | tf_op jit(solution)/shard_map/ppermute | solution.py:24
  13.7 69.2 %collective-permute-start.4 = (bf16[2,384,1536]{2,1,0:T(8,128)(2,1)}, bf16[2,384,1536]{2,1,0:T(8,128)(2,1)}, u32[]{:S(2)}, u32[]{:S(2)}) collective-permute-start(bf16[2,384,1536]{2,1,0:T(8,128)(2,1)} %bitcast.67), channel_id=1, source_target_pairs={{1,0},{2,1},{3,2},{4,3},{5,4},{6,5},{7,6},{8,7},{9,8},{10,9},{11,1... | collective-permute-start | bytes 7077896 | tf_op jit(solution)/shard_map/ppermute | solution.py:26
  354.5 17.6 %collective-permute-start = (bf16[2,128,1536]{2,1,0:T(8,128)(2,1)S(1)}, bf16[2,128,1536]{2,1,0:T(8,128)(2,1)S(1)}, u32[]{:S(2)}, u32[]{:S(2)}) collective-permute-start(bf16[2,128,1536]{2,1,0:T(8,128)(2,1)S(1)} %get-tuple-element.507), channel_id=1, source_target_pairs={{0,1},{1,2},{2,3},{3,4},{4,5},{5,6},{6,7},{7,8},{8,9},{9,10},{10,1... | collective-permute-start | bytes 2359304 | tf_op jit(solution)/shard_map/while/body/eval_jaxpr/ppermute | solution.py:24
  359.0 20.3 %collective-permute-start.1 = (bf16[2,128,1536]{2,1,0:T(8,128)(2,1)S(1)}, bf16[2,128,1536]{2,1,0:T(8,128)(2,1)S(1)}, u32[]{:S(2)}, u32[]{:S(2)}) collective-permute-start(bf16[2,128,1536]{2,1,0:T(8,128)(2,1)S(1)} %get-tuple-element.507), channel_id=1, source_target_pairs={{1,0},{2,1},{3,2},{4,3},{5,4},{6,5},{7,6},{8,7},{9,8},{10,9},{11,1... | collective-permute-start | bytes 2359304 | tf_op jit(solution)/shard_map/while/body/eval_jaxpr/ppermute | solution.py:26
  389.4 14.9 %collective-permute-start = (bf16[2,128,1536]{2,1,0:T(8,128)(2,1)S(1)}, bf16[2,128,1536]{2,1,0:T(8,128)(2,1)S(1)}, u32[]{:S(2)}, u32[]{:S(2)}) collective-permute-start(bf16[2,128,1536]{2,1,0:T(8,128)(2,1)S(1)} %get-tuple-element.507), channel_id=1, source_target_pairs={{0,1},{1,2},{2,3},{3,4},{4,5},{5,6},{6,7},{7,8},{8,9},{9,10},{10,1... | collective-permute-start | bytes 2359304 | tf_op jit(solution)/shard_map/while/body/eval_jaxpr/ppermute | solution.py:24
  391.4 18.3 %collective-permute-start.1 = (bf16[2,128,1536]{2,1,0:T(8,128)(2,1)S(1)}, bf16[2,128,1536]{2,1,0:T(8,128)(2,1)S(1)}, u32[]{:S(2)}, u32[]{:S(2)}) collective-permute-start(bf16[2,128,1536]{2,1,0:T(8,128)(2,1)S(1)} %get-tuple-element.507), channel_id=1, source_target_pairs={{1,0},{2,1},{3,2},{4,3},{5,4},{6,5},{7,6},{8,7},{9,8},{10,9},{11,1... | collective-permute-start | bytes 2359304 | tf_op jit(solution)/shard_map/while/body/eval_jaxpr/ppermute | solution.py:26
  423.8 17.2 %collective-permute-start.1 = (bf16[2,128,1536]{2,1,0:T(8,128)(2,1)S(1)}, bf16[2,128,1536]{2,1,0:T(8,128)(2,1)S(1)}, u32[]{:S(2)}, u32[]{:S(2)}) collective-permute-start(bf16[2,128,1536]{2,1,0:T(8,128)(2,1)S(1)} %get-tuple-element.507), channel_id=1, source_target_pairs={{1,0},{2,1},{3,2},{4,3},{5,4},{6,5},{7,6},{8,7},{9,8},{10,9},{11,1... | collective-permute-start | bytes 2359304 | tf_op jit(solution)/shard_map/while/body/eval_jaxpr/ppermute | solution.py:26
  454.3 14.9 %collective-permute-start = (bf16[2,128,1536]{2,1,0:T(8,128)(2,1)S(1)}, bf16[2,128,1536]{2,1,0:T(8,128)(2,1)S(1)}, u32[]{:S(2)}, u32[]{:S(2)}) collective-permute-start(bf16[2,128,1536]{2,1,0:T(8,128)(2,1)S(1)} %get-tuple-element.507), channel_id=1, source_target_pairs={{0,1},{1,2},{2,3},{3,4},{4,5},{5,6},{6,7},{7,8},{8,9},{9,10},{10,1... | collective-permute-start | bytes 2359304 | tf_op jit(solution)/shard_map/while/body/eval_jaxpr/ppermute | solution.py:24
  456.2 18.3 %collective-permute-start.1 = (bf16[2,128,1536]{2,1,0:T(8,128)(2,1)S(1)}, bf16[2,128,1536]{2,1,0:T(8,128)(2,1)S(1)}, u32[]{:S(2)}, u32[]{:S(2)}) collective-permute-start(bf16[2,128,1536]{2,1,0:T(8,128)(2,1)S(1)} %get-tuple-element.507), channel_id=1, source_target_pairs={{1,0},{2,1},{3,2},{4,3},{5,4},{6,5},{7,6},{8,7},{9,8},{10,9},{11,1... | collective-permute-start | bytes 2359304 | tf_op jit(solution)/shard_map/while/body/eval_jaxpr/ppermute | solution.py:26
  486.7 14.9 %collective-permute-start = (bf16[2,128,1536]{2,1,0:T(8,128)(2,1)S(1)}, bf16[2,128,1536]{2,1,0:T(8,128)(2,1)S(1)}, u32[]{:S(2)}, u32[]{:S(2)}) collective-permute-start(bf16[2,128,1536]{2,1,0:T(8,128)(2,1)S(1)} %get-tuple-element.507), channel_id=1, source_target_pairs={{0,1},{1,2},{2,3},{3,4},{4,5},{5,6},{6,7},{7,8},{8,9},{9,10},{10,1... | collective-permute-start | bytes 2359304 | tf_op jit(solution)/shard_map/while/body/eval_jaxpr/ppermute | solution.py:24
  488.6 18.3 %collective-permute-start.1 = (bf16[2,128,1536]{2,1,0:T(8,128)(2,1)S(1)}, bf16[2,128,1536]{2,1,0:T(8,128)(2,1)S(1)}, u32[]{:S(2)}, u32[]{:S(2)}) collective-permute-start(bf16[2,128,1536]{2,1,0:T(8,128)(2,1)S(1)} %get-tuple-element.507), channel_id=1, source_target_pairs={{1,0},{2,1},{3,2},{4,3},{5,4},{6,5},{7,6},{8,7},{9,8},{10,9},{11,1... | collective-permute-start | bytes 2359304 | tf_op jit(solution)/shard_map/while/body/eval_jaxpr/ppermute | solution.py:26
  521.0 18.3 %collective-permute-start.1 = (bf16[2,128,1536]{2,1,0:T(8,128)(2,1)S(1)}, bf16[2,128,1536]{2,1,0:T(8,128)(2,1)S(1)}, u32[]{:S(2)}, u32[]{:S(2)}) collective-permute-start(bf16[2,128,1536]{2,1,0:T(8,128)(2,1)S(1)} %get-tuple-element.507), channel_id=1, source_target_pairs={{1,0},{2,1},{3,2},{4,3},{5,4},{6,5},{7,6},{8,7},{9,8},{10,9},{11,1... | collective-permute-start | bytes 2359304 | tf_op jit(solution)/shard_map/while/body/eval_jaxpr/ppermute | solution.py:26
  553.4 16.1 %collective-permute-start.1 = (bf16[2,128,1536]{2,1,0:T(8,128)(2,1)S(1)}, bf16[2,128,1536]{2,1,0:T(8,128)(2,1)S(1)}, u32[]{:S(2)}, u32[]{:S(2)}) collective-permute-start(bf16[2,128,1536]{2,1,0:T(8,128)(2,1)S(1)} %get-tuple-element.507), channel_id=1, source_target_pairs={{1,0},{2,1},{3,2},{4,3},{5,4},{6,5},{7,6},{8,7},{9,8},{10,9},{11,1... | collective-permute-start | bytes 2359304 | tf_op jit(solution)/shard_map/while/body/eval_jaxpr/ppermute | solution.py:26
  570.3 420.7 %collective-permute-start.2 = (bf16[128,1536]{1,0:T(8,128)(2,1)}, bf16[128,1536]{1,0:T(8,128)(2,1)S(1)}, u32[]{:S(2)}, u32[]{:S(2)}) collective-permute-start(bf16[128,1536]{1,0:T(8,128)(2,1)} %get-tuple-element.510), channel_id=1, source_target_pairs={{0,32},{32,64},{64,96},{96,128},{128,160},{160,192},{192,224},{1,3... | collective-permute-start | bytes 1179656 | tf_op jit(solution)/shard_map/while/body/eval_jaxpr/ppermute | solution.py:36
  1003.9 16.1 %collective-permute-start.1 = (bf16[2,128,1536]{2,1,0:T(8,128)(2,1)S(1)}, bf16[2,128,1536]{2,1,0:T(8,128)(2,1)S(1)}, u32[]{:S(2)}, u32[]{:S(2)}) collective-permute-start(bf16[2,128,1536]{2,1,0:T(8,128)(2,1)S(1)} %get-tuple-element.507), channel_id=1, source_target_pairs={{1,0},{2,1},{3,2},{4,3},{5,4},{6,5},{7,6},{8,7},{9,8},{10,9},{11,1... | collective-permute-start | bytes 2359304 | tf_op jit(solution)/shard_map/while/body/eval_jaxpr/ppermute | solution.py:26
  1074.0 15.3 %collective-permute-start.2 = (bf16[128,1536]{1,0:T(8,128)(2,1)}, bf16[128,1536]{1,0:T(8,128)(2,1)S(1)}, u32[]{:S(2)}, u32[]{:S(2)}) collective-permute-start(bf16[128,1536]{1,0:T(8,128)(2,1)} %get-tuple-element.510), channel_id=1, source_target_pairs={{0,32},{32,64},{64,96},{96,128},{128,160},{160,192},{192,224},{1,3... | collective-permute-start | bytes 1179656 | tf_op jit(solution)/shard_map/while/body/eval_jaxpr/ppermute | solution.py:36
  1102.2 16.1 %collective-permute-start.1 = (bf16[2,128,1536]{2,1,0:T(8,128)(2,1)S(1)}, bf16[2,128,1536]{2,1,0:T(8,128)(2,1)S(1)}, u32[]{:S(2)}, u32[]{:S(2)}) collective-permute-start(bf16[2,128,1536]{2,1,0:T(8,128)(2,1)S(1)} %get-tuple-element.507), channel_id=1, source_target_pairs={{1,0},{2,1},{3,2},{4,3},{5,4},{6,5},{7,6},{8,7},{9,8},{10,9},{11,1... | collective-permute-start | bytes 2359304 | tf_op jit(solution)/shard_map/while/body/eval_jaxpr/ppermute | solution.py:26
  1172.3 19.4 %collective-permute-start.2 = (bf16[128,1536]{1,0:T(8,128)(2,1)}, bf16[128,1536]{1,0:T(8,128)(2,1)S(1)}, u32[]{:S(2)}, u32[]{:S(2)}) collective-permute-start(bf16[128,1536]{1,0:T(8,128)(2,1)} %get-tuple-element.510), channel_id=1, source_target_pairs={{0,32},{32,64},{64,96},{96,128},{128,160},{160,192},{192,224},{1,3... | collective-permute-start | bytes 1179656 | tf_op jit(solution)/shard_map/while/body/eval_jaxpr/ppermute | solution.py:36
  1202.7 18.1 %collective-permute-start = (bf16[2,128,1536]{2,1,0:T(8,128)(2,1)S(1)}, bf16[2,128,1536]{2,1,0:T(8,128)(2,1)S(1)}, u32[]{:S(2)}, u32[]{:S(2)}) collective-permute-start(bf16[2,128,1536]{2,1,0:T(8,128)(2,1)S(1)} %get-tuple-element.507), channel_id=1, source_target_pairs={{0,1},{1,2},{2,3},{3,4},{4,5},{5,6},{6,7},{7,8},{8,9},{9,10},{10,1... | collective-permute-start | bytes 2359304 | tf_op jit(solution)/shard_map/while/body/eval_jaxpr/ppermute | solution.py:24
  1204.6 21.1 %collective-permute-start.1 = (bf16[2,128,1536]{2,1,0:T(8,128)(2,1)S(1)}, bf16[2,128,1536]{2,1,0:T(8,128)(2,1)S(1)}, u32[]{:S(2)}, u32[]{:S(2)}) collective-permute-start(bf16[2,128,1536]{2,1,0:T(8,128)(2,1)S(1)} %get-tuple-element.507), channel_id=1, source_target_pairs={{1,0},{2,1},{3,2},{4,3},{5,4},{6,5},{7,6},{8,7},{9,8},{10,9},{11,1... | collective-permute-start | bytes 2359304 | tf_op jit(solution)/shard_map/while/body/eval_jaxpr/ppermute | solution.py:26
  (34 other events, 598.7 us)
Sparse Core Ops, SparseCore 0:
  9.9 93.6 all-gather.8
  106.3 79.1 all-gather.10
  188.0 80.7 all-gather.12
  271.3 80.7 all-gather.14
where the time goes:
time: 1290 us
  waiting for transfers between devices  988 us (77%)
  local copies, waits for them, and re-layouts  128 us (10%)
  starting transfers between devices  73.2 us (6%)
  matrix products  52.2 us (4%)
  other arithmetic  34.5 us (3%)
  between operations  13.2 us (1%)
    ppermute x10, waiting for transfers between devices, from_behind(): return lax.ppermute(value, axis, pairs)  507 us
    ppermute x11, waiting for transfers between devices, extended(): lax.ppermute(tail, axis, [(i, (i + 1) % count) for i in range(ends)])  153 us
    all_gather x1, waiting for transfers between devices, per_device(): lax.all_gather(value_weight[0], 'seq', axis=0, tiled=True)  83.4 us
    all_gather x1, waiting for transfers between devices, per_device(): lax.all_gather(out_weight[0], 'seq', axis=0, tiled=True)  83.3 us
    all_gather x1, waiting for transfers between devices, per_device(): lax.all_gather(key_weight[0], 'seq', axis=0, tiled=True)  81.8 us
    ppermute x11, waiting for transfers between devices, extended(): lax.ppermute(head, axis, [((i + 1) % count, i) for i in range(ends)])  62 us
    ppermute x11, starting transfers between devices, extended(): lax.ppermute(head, axis, [((i + 1) % count, i) for i in range(ends)])  34.1 us
    ppermute x11, starting transfers between devices, extended(): lax.ppermute(tail, axis, [(i, (i + 1) % count) for i in range(ends)])  26.1 us
  transfers between devices with their start and end apart: 36, of which 36 were waited for; matrix products, arithmetic and copies ran while one was open for 0% of the time, Pallas kernels for 0%

commit v1 on v0

--- a/solution.py
+++ b/solution.py
@@ -11,6 +11,12 @@
 PATCHES = 3
 TPP = 2
 epsilon = 1e-06
+
+
+def hold_panels_now(vec):
+    mat_out = jnp.concatenate([vec for _ in range(jax.lax.psum(1, "seq"))], 0)
+    reached = jax.lax.all_to_all(mat_out, "seq", 0, 0, tiled=True)
+    return reached
 
 
 def extended(cells, sides, width):
@@ -88,7 +94,7 @@
     rounds = PATCHES + lax.axis_size("segment") - 1
     full_q, full_k, full_v, full_out = (
         lax.all_gather(query_weight[0], "seq", axis=0, tiled=True),
-        lax.all_gather(key_weight[0], "seq", axis=0, tiled=True),
+        hold_panels_now(key_weight[0]),
         lax.all_gather(value_weight[0], "seq", axis=0, tiled=True),
         lax.all_gather(out_weight[0], "seq", axis=0, tiled=True),
     )

time: 1290 us -> 1270 us (0.984)
  waiting for transfers between devices: 988 us -> 938 us
  local copies, waits for them, and re-layouts: 128 us -> 144 us
    ppermute x11, waiting for transfers between devices: 153 us -> 272 us  [extended(): lax.ppermute(tail, axis, [(i, (i + 1) % count) for i in range(ends)])]
    all_gather x1 -> x0, waiting for transfers between devices: 81.8 us -> none  [per_device(): lax.all_gather(key_weight[0], 'seq', axis=0, tiled=True)]
    all_gather x1, waiting for transfers between devices: 83.4 us -> 17 us  [per_device(): lax.all_gather(value_weight[0], 'seq', axis=0, tiled=True)]
    unnamed x2 -> x39, local copies, waits for them, and re-layouts: 0.01 us -> 16.3 us
    all_gather x1, waiting for transfers between devices: 15.1 us -> 0.01 us  [per_device(): lax.all_gather(query_weight[0], 'seq', axis=0, tiled=True)]
  transfers between devices with their start and end apart: 36 -> 36, of which waited for: 36 -> 34; matrix products, arithmetic and copies ran while one was open for 0% -> 2% of each run, Pallas kernels for 0% -> 0%
where the time goes in v1:
time: 1270 us
  waiting for transfers between devices  938 us (74%)
  local copies, waits for them, and re-layouts  144 us (11%)
  starting transfers between devices  82.7 us (7%)
  matrix products  52.4 us (4%)
  other arithmetic  34.6 us (3%)
  between operations  13.4 us (1%)
    ppermute x10, waiting for transfers between devices, from_behind(): return lax.ppermute(value, axis, pairs)  506 us
    ppermute x11, waiting for transfers between devices, extended(): lax.ppermute(tail, axis, [(i, (i + 1) % count) for i in range(ends)])  272 us
    all_gather x1, waiting for transfers between devices, per_device(): lax.all_gather(out_weight[0], 'seq', axis=0, tiled=True)  83.3 us
    ppermute x11, waiting for transfers between devices, extended(): lax.ppermute(head, axis, [((i + 1) % count, i) for i in range(ends)])  56.9 us
    ppermute x11, starting transfers between devices, extended(): lax.ppermute(head, axis, [((i + 1) % count, i) for i in range(ends)])  34.1 us
    ppermute x11, starting transfers between devices, extended(): lax.ppermute(tail, axis, [(i, (i + 1) % count) for i in range(ends)])  26 us
  transfers between devices with their start and end apart: 36, of which 34 were waited for; matrix products, arithmetic and copies ran while one was open for 2% of the time, Pallas kernels for 0%

profile of v1, /device:TPU:127, one launch (start us, length us, event | category | flops | bytes accessed | tf_op | source)
XLA Modules:
  0.0 1266.3 jit_solution(18237520273633556937)
XLA Ops:
  24.5 9.7 all-to-all-start
  41.2 178.7 %collective-permute-done.3 = bf16[2,384,1536]{2,1,0:T(8,128)(2,1)} collective-permute-done((bf16[2,384,1536]{2,1,0:T(8,128)(2,1)S(1)}, bf16[2,384,1536]{2,1,0:T(8,128)(2,1)}, u32[]{:S(2)}, u32[]{:S(2)}) %collective-permute-start.3) | collective-permute-done | bytes 2359328 | tf_op jit(solution)/shard_map/ppermute | solution.py:30
  228.5 17.0 %all-gather.9.cloned.1.call-done = bf16[1,1536,1536]{2,1,0:T(8,128)(2,1)} async-done(((bf16[1,48,1536]{2,1,0:T(8,128)(2,1)}), bf16[1,1536,1536]{2,1,0:T(8,128)(2,1)}) %all-gather.9.cloned.1.call-update) | async-done | bytes 4718608 | tf_op jit(solution)/shard_map/all_gather | solution.py:98
  245.5 83.3 %all-gather.11.cloned.1.call-done = bf16[1,1536,1536]{2,1,0:T(8,128)(2,1)} async-done(((bf16[1,48,1536]{2,1,0:T(8,128)(2,1)}), bf16[1,1536,1536]{2,1,0:T(8,128)(2,1)}) %all-gather.11.cloned.1.call-update) | async-done | bytes 4718608 | tf_op jit(solution)/shard_map/all_gather | solution.py:99
  330.0 929.8 %while.18 = (s32[]{:T(128)}, bf16[2,1152,1536]{2,1,0:T(8,128)(2,1)}, bf16[128,1536]{1,0:T(8,128)(2,1)S(1)}, bf16[384,1536]{1,0:T(8,128)(2,1)}, s32[]{:T(128)}, /...) while((s32[]{:T(128)}, ...), condition=%wide.region_8.10_spmd, body=%wide.region_0.9_spmd.sunk | while | flops 2727545344 | bytes 147957200 | solution.py:152
  337.6 11.2 collective-permute-done
  371.5 9.7 collective-permute-done
  388.4 8.9 collective-permute-done.2
  419.7 10.0 collective-permute-done.2
  436.3 9.7 collective-permute-done
  468.7 9.7 collective-permute-done
  485.7 8.9 collective-permute-done.2
  501.1 9.7 collective-permute-done
  518.1 8.9 collective-permute-done.2
  548.3 418.8 %collective-permute-done.2 = bf16[128,1536]{1,0:T(8,128)(2,1)S(1)} collective-permute-done((bf16[128,1536]{1,0:T(8,128)(2,1)}, bf16[128,1536]{1,0:T(8,128)(2,1)S(1)}, u32[]{:S(2)}, u32[]{:S(2)}) %collective-permute-start.2) | collective-permute-done | bytes 393248 | tf_op jit(solution)/shard_map/while/body/eval_jaxpr/ppermute | solution.py:42
  968.2 9.8 conditional.4
  995.9 54.0 %conditional.5 = (bf16[2,1152,1536]{2,1,0:T(8,128)(2,1)}, bf16[384,1536]{1,0:T(8,128)(2,1)}, bf16[128,1536]{1,0:T(8,128)(2,1)}) conditional(s32[]{:T(128)} %convert_element_type.58, (bf16[2,1152,1536]{2,1,0:T(8,128)(2,1)}, bf16[384,1536]{1,0:T(8,128)(2,1)}) %tuple.60, (s32[]{:T(128)}, bf16[2,1152,1536]{2,1,0:T(8,128)(2,1)}, ...), branch_computations={%region_5.5_spmd, %region_6.8_spmd} | conditional | flops 912850560 | bytes 86146920 | solution.py:147
  1051.2 13.9 %collective-permute-done.2 = bf16[128,1536]{1,0:T(8,128)(2,1)S(1)} collective-permute-done((bf16[128,1536]{1,0:T(8,128)(2,1)}, bf16[128,1536]{1,0:T(8,128)(2,1)S(1)}, u32[]{:S(2)}, u32[]{:S(2)}) %collective-permute-start.2) | collective-permute-done | bytes 393248 | tf_op jit(solution)/shard_map/while/body/eval_jaxpr/ppermute | solution.py:42
  1066.2 9.8 conditional.4
  1093.9 54.1 %conditional.5 = (bf16[2,1152,1536]{2,1,0:T(8,128)(2,1)}, bf16[384,1536]{1,0:T(8,128)(2,1)}, bf16[128,1536]{1,0:T(8,128)(2,1)}) conditional(s32[]{:T(128)} %convert_element_type.58, (bf16[2,1152,1536]{2,1,0:T(8,128)(2,1)}, bf16[384,1536]{1,0:T(8,128)(2,1)}) %tuple.60, (s32[]{:T(128)}, bf16[2,1152,1536]{2,1,0:T(8,128)(2,1)}, ...), branch_computations={%region_5.5_spmd, %region_6.8_spmd} | conditional | flops 912850560 | bytes 86146920 | solution.py:147
  1149.3 18.7 %collective-permute-done.2 = bf16[128,1536]{1,0:T(8,128)(2,1)S(1)} collective-permute-done((bf16[128,1536]{1,0:T(8,128)(2,1)}, bf16[128,1536]{1,0:T(8,128)(2,1)S(1)}, u32[]{:S(2)}, u32[]{:S(2)}) %collective-permute-start.2) | collective-permute-done | bytes 393248 | tf_op jit(solution)/shard_map/while/body/eval_jaxpr/ppermute | solution.py:42
  1169.1 9.8 conditional.4
  1184.2 12.9 %collective-permute-done = bf16[2,128,1536]{2,1,0:T(8,128)(2,1)S(1)} collective-permute-done((bf16[2,128,1536]{2,1,0:T(8,128)(2,1)S(1)}, bf16[2,128,1536]{2,1,0:T(8,128)(2,1)S(1)}, u32[]{:S(2)}, u32[]{:S(2)}) %collective-permute-start) | collective-permute-done | bytes 786464 | tf_op jit(solution)/shard_map/while/body/eval_jaxpr/ppermute | solution.py:30
  1202.1 53.9 %conditional.5 = (bf16[2,1152,1536]{2,1,0:T(8,128)(2,1)}, bf16[384,1536]{1,0:T(8,128)(2,1)}, bf16[128,1536]{1,0:T(8,128)(2,1)}) conditional(s32[]{:T(128)} %convert_element_type.58, (bf16[2,1152,1536]{2,1,0:T(8,128)(2,1)}, bf16[384,1536]{1,0:T(8,128)(2,1)}) %tuple.60, (s32[]{:T(128)}, bf16[2,1152,1536]{2,1,0:T(8,128)(2,1)}, ...), branch_computations={%region_5.5_spmd, %region_6.8_spmd} | conditional | flops 912850560 | bytes 86146920 | solution.py:147
  (305 shorter events, 418.2 us)
Async XLA Ops:
  6.5 221.9 %all-gather.7.cloned.1.call-start = ((), (), s32[]{:S(2)}) async-start(), calls=%async_computation.1 | async-start | bytes 4866048 | tf_op jit(solution)/shard_map/all_gather | solution.py:96
  7.3 238.2 %all-gather.9.cloned.1.call-start = ((), (), s32[]{:S(2)}) async-start(), calls=%async_computation.2 | async-start | bytes 4866048 | tf_op jit(solution)/shard_map/all_gather | solution.py:98
  24.5 204.0 %all-to-all-start = ((bf16[32,48,1536]{2,1,0:T(8,128)(2,1)}), bf16[32,48,1536]{2,1,0:T(8,128)(2,1)}, u32[]{:S(2)}, u32[]{:S(2)}) async-start(bf16[32,48,1536]{2,1,0:T(8,128)(2,1)} %bitcast.99), calls=%async_computation | async-start | bytes 9437184 | tf_op jit(solution)/shard_map/all_to_all | solution.py:18
  34.2 294.6 %all-gather.11.cloned.1.call-start = ((), (), s32[]{:S(2)}) async-start(), calls=%async_computation.3 | async-start | bytes 4866048 | tf_op jit(solution)/shard_map/all_gather | solution.py:99
  35.0 184.9 %collective-permute-start.3 = (bf16[2,384,1536]{2,1,0:T(8,128)(2,1)S(1)}, bf16[2,384,1536]{2,1,0:T(8,128)(2,1)}, u32[]{:S(2)}, u32[]{:S(2)}) collective-permute-start(bf16[2,384,1536]{2,1,0:T(8,128)(2,1)S(1)} %bitcast.100), channel_id=1, source_target_pairs={{0,1},{1,2},{2,3},{3,4},{4,5},{5,6},{6,7},{7,8},{8,9},{9,10},{10,1... | collective-permute-start | bytes 7077896 | tf_op jit(solution)/shard_map/ppermute | solution.py:30
  39.3 183.4 %collective-permute-start.4 = (bf16[2,384,1536]{2,1,0:T(8,128)(2,1)S(1)}, bf16[2,384,1536]{2,1,0:T(8,128)(2,1)}, u32[]{:S(2)}, u32[]{:S(2)}) collective-permute-start(bf16[2,384,1536]{2,1,0:T(8,128)(2,1)S(1)} %bitcast.101), channel_id=1, source_target_pairs={{1,0},{2,1},{3,2},{4,3},{5,4},{6,5},{7,6},{8,7},{9,8},{10,9},{11,1... | collective-permute-start | bytes 7077896 | tf_op jit(solution)/shard_map/ppermute | solution.py:32
  331.2 17.6 %collective-permute-start = (bf16[2,128,1536]{2,1,0:T(8,128)(2,1)S(1)}, bf16[2,128,1536]{2,1,0:T(8,128)(2,1)S(1)}, u32[]{:S(2)}, u32[]{:S(2)}) collective-permute-start(bf16[2,128,1536]{2,1,0:T(8,128)(2,1)S(1)} %get-tuple-element.507), channel_id=1, source_target_pairs={{0,1},{1,2},{2,3},{3,4},{4,5},{5,6},{6,7},{7,8},{8,9},{9,10},{10,1... | collective-permute-start | bytes 2359304 | tf_op jit(solution)/shard_map/while/body/eval_jaxpr/ppermute | solution.py:30
  335.7 20.3 %collective-permute-start.1 = (bf16[2,128,1536]{2,1,0:T(8,128)(2,1)S(1)}, bf16[2,128,1536]{2,1,0:T(8,128)(2,1)S(1)}, u32[]{:S(2)}, u32[]{:S(2)}) collective-permute-start(bf16[2,128,1536]{2,1,0:T(8,128)(2,1)S(1)} %get-tuple-element.507), channel_id=1, source_target_pairs={{1,0},{2,1},{3,2},{4,3},{5,4},{6,5},{7,6},{8,7},{9,8},{10,9},{11,1... | collective-permute-start | bytes 2359304 | tf_op jit(solution)/shard_map/while/body/eval_jaxpr/ppermute | solution.py:32
  366.2 14.9 %collective-permute-start = (bf16[2,128,1536]{2,1,0:T(8,128)(2,1)S(1)}, bf16[2,128,1536]{2,1,0:T(8,128)(2,1)S(1)}, u32[]{:S(2)}, u32[]{:S(2)}) collective-permute-start(bf16[2,128,1536]{2,1,0:T(8,128)(2,1)S(1)} %get-tuple-element.507), channel_id=1, source_target_pairs={{0,1},{1,2},{2,3},{3,4},{4,5},{5,6},{6,7},{7,8},{8,9},{9,10},{10,1... | collective-permute-start | bytes 2359304 | tf_op jit(solution)/shard_map/while/body/eval_jaxpr/ppermute | solution.py:30
  368.1 18.3 %collective-permute-start.1 = (bf16[2,128,1536]{2,1,0:T(8,128)(2,1)S(1)}, bf16[2,128,1536]{2,1,0:T(8,128)(2,1)S(1)}, u32[]{:S(2)}, u32[]{:S(2)}) collective-permute-start(bf16[2,128,1536]{2,1,0:T(8,128)(2,1)S(1)} %get-tuple-element.507), channel_id=1, source_target_pairs={{1,0},{2,1},{3,2},{4,3},{5,4},{6,5},{7,6},{8,7},{9,8},{10,9},{11,1... | collective-permute-start | bytes 2359304 | tf_op jit(solution)/shard_map/while/body/eval_jaxpr/ppermute | solution.py:32
  400.5 17.2 %collective-permute-start.1 = (bf16[2,128,1536]{2,1,0:T(8,128)(2,1)S(1)}, bf16[2,128,1536]{2,1,0:T(8,128)(2,1)S(1)}, u32[]{:S(2)}, u32[]{:S(2)}) collective-permute-start(bf16[2,128,1536]{2,1,0:T(8,128)(2,1)S(1)} %get-tuple-element.507), channel_id=1, source_target_pairs={{1,0},{2,1},{3,2},{4,3},{5,4},{6,5},{7,6},{8,7},{9,8},{10,9},{11,1... | collective-permute-start | bytes 2359304 | tf_op jit(solution)/shard_map/while/body/eval_jaxpr/ppermute | solution.py:32
  431.0 14.9 %collective-permute-start = (bf16[2,128,1536]{2,1,0:T(8,128)(2,1)S(1)}, bf16[2,128,1536]{2,1,0:T(8,128)(2,1)S(1)}, u32[]{:S(2)}, u32[]{:S(2)}) collective-permute-start(bf16[2,128,1536]{2,1,0:T(8,128)(2,1)S(1)} %get-tuple-element.507), channel_id=1, source_target_pairs={{0,1},{1,2},{2,3},{3,4},{4,5},{5,6},{6,7},{7,8},{8,9},{9,10},{10,1... | collective-permute-start | bytes 2359304 | tf_op jit(solution)/shard_map/while/body/eval_jaxpr/ppermute | solution.py:30
  432.9 18.3 %collective-permute-start.1 = (bf16[2,128,1536]{2,1,0:T(8,128)(2,1)S(1)}, bf16[2,128,1536]{2,1,0:T(8,128)(2,1)S(1)}, u32[]{:S(2)}, u32[]{:S(2)}) collective-permute-start(bf16[2,128,1536]{2,1,0:T(8,128)(2,1)S(1)} %get-tuple-element.507), channel_id=1, source_target_pairs={{1,0},{2,1},{3,2},{4,3},{5,4},{6,5},{7,6},{8,7},{9,8},{10,9},{11,1... | collective-permute-start | bytes 2359304 | tf_op jit(solution)/shard_map/while/body/eval_jaxpr/ppermute | solution.py:32
  465.3 18.3 %collective-permute-start.1 = (bf16[2,128,1536]{2,1,0:T(8,128)(2,1)S(1)}, bf16[2,128,1536]{2,1,0:T(8,128)(2,1)S(1)}, u32[]{:S(2)}, u32[]{:S(2)}) collective-permute-start(bf16[2,128,1536]{2,1,0:T(8,128)(2,1)S(1)} %get-tuple-element.507), channel_id=1, source_target_pairs={{1,0},{2,1},{3,2},{4,3},{5,4},{6,5},{7,6},{8,7},{9,8},{10,9},{11,1... | collective-permute-start | bytes 2359304 | tf_op jit(solution)/shard_map/while/body/eval_jaxpr/ppermute | solution.py:32
  495.8 14.9 %collective-permute-start = (bf16[2,128,1536]{2,1,0:T(8,128)(2,1)S(1)}, bf16[2,128,1536]{2,1,0:T(8,128)(2,1)S(1)}, u32[]{:S(2)}, u32[]{:S(2)}) collective-permute-start(bf16[2,128,1536]{2,1,0:T(8,128)(2,1)S(1)} %get-tuple-element.507), channel_id=1, source_target_pairs={{0,1},{1,2},{2,3},{3,4},{4,5},{5,6},{6,7},{7,8},{8,9},{9,10},{10,1... | collective-permute-start | bytes 2359304 | tf_op jit(solution)/shard_map/while/body/eval_jaxpr/ppermute | solution.py:30
  497.7 18.3 %collective-permute-start.1 = (bf16[2,128,1536]{2,1,0:T(8,128)(2,1)S(1)}, bf16[2,128,1536]{2,1,0:T(8,128)(2,1)S(1)}, u32[]{:S(2)}, u32[]{:S(2)}) collective-permute-start(bf16[2,128,1536]{2,1,0:T(8,128)(2,1)S(1)} %get-tuple-element.507), channel_id=1, source_target_pairs={{1,0},{2,1},{3,2},{4,3},{5,4},{6,5},{7,6},{8,7},{9,8},{10,9},{11,1... | collective-permute-start | bytes 2359304 | tf_op jit(solution)/shard_map/while/body/eval_jaxpr/ppermute | solution.py:32
  530.1 16.1 %collective-permute-start.1 = (bf16[2,128,1536]{2,1,0:T(8,128)(2,1)S(1)}, bf16[2,128,1536]{2,1,0:T(8,128)(2,1)S(1)}, u32[]{:S(2)}, u32[]{:S(2)}) collective-permute-start(bf16[2,128,1536]{2,1,0:T(8,128)(2,1)S(1)} %get-tuple-element.507), channel_id=1, source_target_pairs={{1,0},{2,1},{3,2},{4,3},{5,4},{6,5},{7,6},{8,7},{9,8},{10,9},{11,1... | collective-permute-start | bytes 2359304 | tf_op jit(solution)/shard_map/while/body/eval_jaxpr/ppermute | solution.py:32
  547.0 420.1 %collective-permute-start.2 = (bf16[128,1536]{1,0:T(8,128)(2,1)}, bf16[128,1536]{1,0:T(8,128)(2,1)S(1)}, u32[]{:S(2)}, u32[]{:S(2)}) collective-permute-start(bf16[128,1536]{1,0:T(8,128)(2,1)} %get-tuple-element.510), channel_id=1, source_target_pairs={{0,32},{32,64},{64,96},{96,128},{128,160},{160,192},{192,224},{1,3... | collective-permute-start | bytes 1179656 | tf_op jit(solution)/shard_map/while/body/eval_jaxpr/ppermute | solution.py:42
  979.8 16.1 %collective-permute-start.1 = (bf16[2,128,1536]{2,1,0:T(8,128)(2,1)S(1)}, bf16[2,128,1536]{2,1,0:T(8,128)(2,1)S(1)}, u32[]{:S(2)}, u32[]{:S(2)}) collective-permute-start(bf16[2,128,1536]{2,1,0:T(8,128)(2,1)S(1)} %get-tuple-element.507), channel_id=1, source_target_pairs={{1,0},{2,1},{3,2},{4,3},{5,4},{6,5},{7,6},{8,7},{9,8},{10,9},{11,1... | collective-permute-start | bytes 2359304 | tf_op jit(solution)/shard_map/while/body/eval_jaxpr/ppermute | solution.py:32
  1049.9 15.2 %collective-permute-start.2 = (bf16[128,1536]{1,0:T(8,128)(2,1)}, bf16[128,1536]{1,0:T(8,128)(2,1)S(1)}, u32[]{:S(2)}, u32[]{:S(2)}) collective-permute-start(bf16[128,1536]{1,0:T(8,128)(2,1)} %get-tuple-element.510), channel_id=1, source_target_pairs={{0,32},{32,64},{64,96},{96,128},{128,160},{160,192},{192,224},{1,3... | collective-permute-start | bytes 1179656 | tf_op jit(solution)/shard_map/while/body/eval_jaxpr/ppermute | solution.py:42
  1077.9 16.1 %collective-permute-start.1 = (bf16[2,128,1536]{2,1,0:T(8,128)(2,1)S(1)}, bf16[2,128,1536]{2,1,0:T(8,128)(2,1)S(1)}, u32[]{:S(2)}, u32[]{:S(2)}) collective-permute-start(bf16[2,128,1536]{2,1,0:T(8,128)(2,1)S(1)} %get-tuple-element.507), channel_id=1, source_target_pairs={{1,0},{2,1},{3,2},{4,3},{5,4},{6,5},{7,6},{8,7},{9,8},{10,9},{11,1... | collective-permute-start | bytes 2359304 | tf_op jit(solution)/shard_map/while/body/eval_jaxpr/ppermute | solution.py:32
  1148.0 20.0 %collective-permute-start.2 = (bf16[128,1536]{1,0:T(8,128)(2,1)}, bf16[128,1536]{1,0:T(8,128)(2,1)S(1)}, u32[]{:S(2)}, u32[]{:S(2)}) collective-permute-start(bf16[128,1536]{1,0:T(8,128)(2,1)} %get-tuple-element.510), channel_id=1, source_target_pairs={{0,32},{32,64},{64,96},{96,128},{128,160},{160,192},{192,224},{1,3... | collective-permute-start | bytes 1179656 | tf_op jit(solution)/shard_map/while/body/eval_jaxpr/ppermute | solution.py:42
  1178.9 18.2 %collective-permute-start = (bf16[2,128,1536]{2,1,0:T(8,128)(2,1)S(1)}, bf16[2,128,1536]{2,1,0:T(8,128)(2,1)S(1)}, u32[]{:S(2)}, u32[]{:S(2)}) collective-permute-start(bf16[2,128,1536]{2,1,0:T(8,128)(2,1)S(1)} %get-tuple-element.507), channel_id=1, source_target_pairs={{0,1},{1,2},{2,3},{3,4},{4,5},{5,6},{6,7},{7,8},{8,9},{9,10},{10,1... | collective-permute-start | bytes 2359304 | tf_op jit(solution)/shard_map/while/body/eval_jaxpr/ppermute | solution.py:30
  1180.8 21.3 %collective-permute-start.1 = (bf16[2,128,1536]{2,1,0:T(8,128)(2,1)S(1)}, bf16[2,128,1536]{2,1,0:T(8,128)(2,1)S(1)}, u32[]{:S(2)}, u32[]{:S(2)}) collective-permute-start(bf16[2,128,1536]{2,1,0:T(8,128)(2,1)S(1)} %get-tuple-element.507), channel_id=1, source_target_pairs={{1,0},{2,1},{3,2},{4,3},{5,4},{6,5},{7,6},{8,7},{9,8},{10,9},{11,1... | collective-permute-start | bytes 2359304 | tf_op jit(solution)/shard_map/while/body/eval_jaxpr/ppermute | solution.py:32
  (37 other events, 579.7 us)
Sparse Core Ops, SparseCore 0:
  9.9 143.8 all-gather.6
  156.4 89.0 all-gather.8
  248.1 80.7 all-gather.10
